TPU v7x, 256 devices: a whole 4x4x8 slice. The times are simulated.
256 devices in a mesh: gx: 8 (over y, core), gy: 32 (over x, z).
Axes of the slice: x: 4, y: 4, z: 8, core: 2. Of those that a mesh axis runs over, the one named last changes fastest.
Arguments:
- flow_field: float32 [16, 256, 256, 128], P(None, 'gx', 'gy'), may hold values from -6 to 6
- cotangent: float32 [16, 256, 256, 128], P(None, 'gx', 'gy'), may hold values from -6 to 6
- mode_weights: float32 [4, 16, 16, 256], replicated, may hold values from -3 to 3
- point_weights: float32 [16, 16], replicated, may hold values from -1.5 to 1.5
- point_bias: float32 [16], replicated, may hold values from -3 to 3
Outputs:
- output_field: float32 [16, 256, 256, 128], P(None, 'gx', 'gy')
- grad_field: float32 [16, 256, 256, 128], P(None, 'gx', 'gy')
- grad_modes: float32 [4, 16, 16, 256], replicated
- grad_point: float32 [16, 16], replicated
- grad_bias: float32 [16], replicated
All inputs are finite; a program needn't handle non-finite values.
Results may differ from a plain program's by a relative error of at most 0.00024.
Values sent between devices are 32-bit elements; how exact they have to be, the bound alone decides.
No kernel may reach another device: no remote copies, remote signals or barrier semaphores. Data moves between devices by JAX's collectives and lax.ppermute only.
A program may use at most 128 MiB of HBM per device.

v0:
```python
import math
import jax
import jax.numpy as jnp
from jax import lax
from jax.sharding import PartitionSpec as P

LOW_PASS = [
    0.23037781330885523,
    0.7148465705525415,
    0.6308807679295904,
    -0.02798376941698385,
    -0.18703481171888114,
    0.030841381835986965,
    0.032883011666982945,
    -0.010597401784997278,
]
HIGH_PASS = [(-1) ** position * LOW_PASS[7 - position] for position in range(8)]
GELU_SCALE = 0.7978845608028654
GELU_CUBE = 0.044715


def from_behind(value, axis, by):
    devices = lax.axis_size(axis)
    return lax.ppermute(value, axis, [(i, (i + by) % devices) for i in range(devices)])


def filter_table(filter_taps, out_count, in_count, periodic):
    row_index = lax.broadcasted_iota(jnp.int32, (out_count, in_count), 0)
    col_index = lax.broadcasted_iota(jnp.int32, (out_count, in_count), 1)
    offset = col_index - 2 * row_index
    if periodic:
        offset = offset % in_count
    matrix = jnp.zeros((out_count, in_count), jnp.float32)
    for position in range(8):
        matrix = matrix + filter_taps[position] * (offset == position).astype(jnp.float32)
    return matrix


def lifted_table(filter_taps, out_count, in_count):
    row_index = lax.broadcasted_iota(jnp.int32, (out_count, in_count), 0)
    col_index = lax.broadcasted_iota(jnp.int32, (out_count, in_count), 1)
    offset = row_index - 2 * col_index + 6
    matrix = jnp.zeros((out_count, in_count), jnp.float32)
    for position in range(8):
        matrix = matrix + filter_taps[position] * (offset == position).astype(jnp.float32)
    return matrix


def along_x(matrix, signal):
    return jnp.einsum("kr,arys->akys", matrix, signal, precision=lax.Precision.HIGHEST)


def along_y(matrix, signal):
    return jnp.einsum("kr,axrs->axks", matrix, signal, precision=lax.Precision.HIGHEST)


def plane_x(matrix, signal):
    return jnp.einsum("kr,ary->aky", matrix, signal, precision=lax.Precision.HIGHEST)


def plane_y(matrix, signal):
    return jnp.einsum("kr,axr->axk", matrix, signal, precision=lax.Precision.HIGHEST)


def to_lanes(signal):
    channels, extent_x, extent_y, planes = signal.shape
    return jnp.transpose(signal, (0, 3, 1, 2)).reshape(channels * planes, extent_x, extent_y)


def from_lanes(signal, channels):
    stacked, extent_x, extent_y = signal.shape
    return jnp.transpose(
        signal.reshape(channels, stacked // channels, extent_x, extent_y), (0, 2, 3, 1)
    )


def four_bands(signal):
    extent_x, extent_y = (signal.shape[1], signal.shape[2])
    low_x = plane_x(filter_table(LOW_PASS, extent_x // 2, extent_x, True), signal)
    high_x = plane_x(filter_table(HIGH_PASS, extent_x // 2, extent_x, True), signal)
    low_y = filter_table(LOW_PASS, extent_y // 2, extent_y, True)
    high_y = filter_table(HIGH_PASS, extent_y // 2, extent_y, True)
    return jnp.stack(
        [
            plane_y(low_y, low_x),
            plane_y(low_y, high_x),
            plane_y(high_y, low_x),
            plane_y(high_y, high_x),
        ]
    )


def join_bands(changes):
    modes_x, modes_y = (changes.shape[2], changes.shape[3])
    low_x = filter_table(LOW_PASS, modes_x, 2 * modes_x, True).T
    high_x = filter_table(HIGH_PASS, modes_x, 2 * modes_x, True).T
    low_y = filter_table(LOW_PASS, modes_y, 2 * modes_y, True).T
    high_y = filter_table(HIGH_PASS, modes_y, 2 * modes_y, True).T
    from_low = plane_y(low_y, changes[0]) + plane_y(high_y, changes[2])
    from_high = plane_y(low_y, changes[1]) + plane_y(high_y, changes[3])
    return plane_x(low_x, from_low) + plane_x(high_x, from_high)


def gelu_parts(signal):
    tangent = jnp.tanh(GELU_SCALE * (signal + GELU_CUBE * signal * signal * signal))
    activated = 0.5 * signal * (1.0 + tangent)
    gelu_slope = 0.5 * (1.0 + tangent) + 0.5 * signal * (1.0 - tangent * tangent) * GELU_SCALE * (
        1.0 + 3.0 * GELU_CUBE * signal * signal
    )
    return (activated, gelu_slope)


def wave_block(signal, weights_grid, transposed):
    x_index = lax.axis_index("gx")
    channels = signal.shape[0]
    extent_x, extent_y = (signal.shape[1], signal.shape[2])
    margin = from_behind(signal[:, :6], "gx", -1)
    halved = along_x(
        filter_table(LOW_PASS, extent_x // 2, extent_x + 6, False),
        jnp.concatenate([signal, margin], 1),
    )
    margin = from_behind(halved[:, :, :6], "gy", -1)
    level_one = along_y(
        filter_table(LOW_PASS, extent_y // 2, extent_y + 6, False),
        jnp.concatenate([halved, margin], 2),
    )
    level_one = to_lanes(lax.all_to_all(level_one, "gy", split_axis=3, concat_axis=2, tiled=True))
    rows_one, cols_one = (level_one.shape[1], level_one.shape[2])
    margin = from_behind(level_one[:, :6], "gx", -1)
    level_two = plane_x(
        filter_table(LOW_PASS, rows_one // 2, rows_one + 6, False),
        jnp.concatenate([level_one, margin], 1),
    )
    level_two = plane_y(filter_table(LOW_PASS, cols_one // 2, cols_one, True), level_two)
    rows_two, cols_two = (level_two.shape[1], level_two.shape[2])
    margin = from_behind(level_two[:, :6], "gx", -1)
    level_three = plane_x(
        filter_table(LOW_PASS, rows_two // 2, rows_two + 6, False),
        jnp.concatenate([level_two, margin], 1),
    )
    level_three = plane_y(filter_table(LOW_PASS, cols_two // 2, cols_two, True), level_three)
    gathered = lax.all_gather(level_three, "gx", axis=1, tiled=True)
    wave_bands = four_bands(gathered)
    stacked, modes_x, modes_y = (wave_bands.shape[1], wave_bands.shape[2], wave_bands.shape[3])
    split_bands = wave_bands.reshape(4, channels, stacked // channels, modes_x, modes_y)
    if transposed:
        mixed_bands = jnp.einsum(
            "bozxy,bioxy->bizxy", split_bands, weights_grid, precision=lax.Precision.HIGHEST
        )
    else:
        mixed_bands = jnp.einsum(
            "bizxy,bioxy->bozxy", split_bands, weights_grid, precision=lax.Precision.HIGHEST
        )
    delta_three = join_bands((mixed_bands - split_bands).reshape(4, stacked, modes_x, modes_y))
    own_rows = rows_two // 2
    own_part = lax.dynamic_slice_in_dim(delta_three, x_index * own_rows, own_rows, 1)
    margin = from_behind(own_part[:, own_rows - 3 :], "gx", 1)
    delta_two = plane_x(
        lifted_table(LOW_PASS, 2 * own_rows, own_rows + 3), jnp.concatenate([margin, own_part], 1)
    )
    cols_three = own_part.shape[2]
    delta_two = plane_y(filter_table(LOW_PASS, cols_three, 2 * cols_three, True).T, delta_two)
    margin = from_behind(delta_two[:, rows_two - 3 :], "gx", 1)
    delta_one = plane_x(
        lifted_table(LOW_PASS, 2 * rows_two, rows_two + 3), jnp.concatenate([margin, delta_two], 1)
    )
    delta_one = plane_y(filter_table(LOW_PASS, cols_two, 2 * cols_two, True).T, delta_one)
    returned = lax.all_to_all(
        from_lanes(delta_one, channels), "gy", split_axis=2, concat_axis=3, tiled=True
    )
    rows_back = returned.shape[1]
    margin = from_behind(returned[:, rows_back - 3 :], "gx", 1)
    widened = along_x(
        lifted_table(LOW_PASS, 2 * rows_back, rows_back + 3), jnp.concatenate([margin, returned], 1)
    )
    cols_back = widened.shape[2]
    margin = from_behind(widened[:, :, cols_back - 3 :], "gy", 1)
    delta_zero = along_y(
        lifted_table(LOW_PASS, 2 * cols_back, cols_back + 3), jnp.concatenate([margin, widened], 2)
    )
    return (signal + delta_zero, split_bands)


def local(flow_field, cotangent, mode_weights, point_weights, point_bias):
    channels = flow_field.shape[0]
    modes_x = flow_field.shape[1] * lax.axis_size("gx") // 16
    modes_y = flow_field.shape[2] * lax.axis_size("gy") // 16
    weights_grid = mode_weights.reshape(4, channels, channels, modes_x, modes_y)
    spectral_flow, bands_flow = wave_block(flow_field, weights_grid, False)
    pointwise = jnp.einsum(
        "io,ixys->oxys", point_weights, flow_field, precision=lax.Precision.HIGHEST
    )
    before_gelu = spectral_flow + pointwise + point_bias[:, None, None, None]
    output_field, gelu_slope = gelu_parts(before_gelu)
    grad_inner = cotangent * gelu_slope
    spectral_grad, bands_grad = wave_block(grad_inner, weights_grid, True)
    point_back = jnp.einsum(
        "io,oxys->ixys", point_weights, grad_inner, precision=lax.Precision.HIGHEST
    )
    grad_field = spectral_grad + point_back
    mode_local = jnp.einsum(
        "bizxy,bozxy->bioxy", bands_flow, bands_grad, precision=lax.Precision.HIGHEST
    )
    mode_local = mode_local.reshape(4, channels, channels, modes_x * modes_y)
    mode_total = lax.psum(mode_local, "gy")
    point_local = jnp.einsum(
        "ixys,oxys->io", flow_field, grad_inner, precision=lax.Precision.HIGHEST
    )
    bias_local = jnp.sum(grad_inner, axis=(1, 2, 3))
    point_total, bias_total = lax.psum((point_local, bias_local), ("gx", "gy"))
    plane_total = flow_field.shape[3]
    cell_count = (
        plane_total
        * flow_field.shape[1]
        * flow_field.shape[2]
        * lax.axis_size("gx")
        * lax.axis_size("gy")
    )
    grad_modes = mode_total / math.sqrt(plane_total)
    grad_point = point_total / math.sqrt(cell_count)
    grad_bias = bias_total / math.sqrt(cell_count)
    return (output_field, grad_field, grad_modes, grad_point, grad_bias)


def solution(mesh):
    in_specs = (P(None, "gx", "gy", None), P(None, "gx", "gy", None), P(), P(), P())
    out_specs = (P(None, "gx", "gy", None), P(None, "gx", "gy", None), P(), P(), P())
    return jax.shard_map(local, mesh=mesh, in_specs=in_specs, out_specs=out_specs, check_vma=False)
```

profile of v0, /device:TPU:8, one launch (start us, length us, event | category | flops | bytes accessed | tf_op | source)
XLA Modules:
  0.0 609.2 jit_solution(3356555167298708479)
XLA Ops:
  7.2 2.0 copy.207
  9.3 6.7 %collective-permute-done = f32[16,6,8,128]{3,1,2,0:T(8,128)S(1)} collective-permute-done((f32[16,6,8,128]{3,1,2,0:T(8,128)S(1)}, f32[16,6,8,128]{3,1,2,0:T(8,128)S(1)}, u32[]{:S(2)}, u32[]{:S(2)}) %collective-permute-start) | collective-permute-done | bytes 393248 | tf_op jit(solution)/shard_map/ppermute | solution.py:24
  17.9 8.1 %collective-permute-start.1 = (f32[16,16,6,128]{3,1,2,0:T(8,128)S(1)}, f32[16,16,6,128]{3,1,2,0:T(8,128)S(1)}, u32[]{:S(2)}, u32[]{:S(2)}) collective-permute-start(f32[16,16,6,128]{3,1,2,0:T(8,128)S(1)} %slice.105), channel_id=1, source_target_pairs={{0,31},{1,0},{2,1},{3,2},{4,3},{5,4},{6,5},{7,6},{8,7},{9,8},{10,9... | collective-permute-start | bytes 2359304 | tf_op jit(solution)/shard_map/ppermute | solution.py:24
  26.0 17.1 %collective-permute-done.1 = f32[16,16,6,128]{3,1,2,0:T(8,128)S(1)} collective-permute-done((f32[16,16,6,128]{3,1,2,0:T(8,128)S(1)}, f32[16,16,6,128]{3,1,2,0:T(8,128)S(1)}, u32[]{:S(2)}, u32[]{:S(2)}) %collective-permute-start.1) | collective-permute-done | bytes 786464 | tf_op jit(solution)/shard_map/ppermute | solution.py:24
  43.2 2.1 fusion.39
  45.4 4.4 copy.209
  49.8 4.3 reshape.86
  54.1 7.6 %all-to-all-start = ((f32[32,1,4096]{2,1,0:T(1,128)}), f32[32,1,4096]{2,1,0:T(1,128)S(1)}, u32[]{:S(2)}, u32[]{:S(2)}) async-start(f32[32,1,4096]{2,1,0:T(1,128)} %reshape.86), calls=%async_computation | async-start | bytes 1048576 | tf_op jit(solution)/shard_map/all_to_all | solution.py:127
  61.7 6.2 %copy.304 = f32[4,16,16,256]{2,1,3,0:T(8,128)} copy(f32[4,16,16,256]{3,2,1,0:T(8,128)S(1)} %copy-done.4) | data formatting | bytes 2097152 | tf_op jit(solution)/shard_map/reshape | solution.py:188
  68.0 11.4 %all-to-all-done = f32[32,1,4096]{2,1,0:T(1,128)S(1)} async-done(((f32[32,1,4096]{2,1,0:T(1,128)}), f32[32,1,4096]{2,1,0:T(1,128)S(1)}, u32[]{:S(2)}, u32[]{:S(2)}) %all-to-all-start) | async-done | bytes 524320 | tf_op jit(solution)/shard_map/all_to_all | solution.py:127
  81.8 2.8 reshape.87
  84.6 4.8 copy.211
  89.4 3.7 copy.212
  93.2 3.9 collective-permute-done.2
  100.1 3.9 collective-permute-done.3
  105.0 14.3 %all_gather.6 = f32[64,32,32]{0,2,1:T(8,128)S(1)} all-gather(f32[64,4,32]{0,2,1:T(8,128)S(1)} %fusion.123), channel_id=1, replica_groups=mesh['gx'=8,'gy'=32] {'gx'}, dimensions={1}, use_global_device_ids=true | all-gather | bytes 294912 | tf_op jit(solution)/shard_map/all_gather | solution.py:142
  125.7 14.9 %bitcast_subtract_fusion.1 = f32[4,16,4,16,16]{1,2,4,3,0:T(4,128)S(1)} fusion(f32[4,16,16,16,16]{2,1,4,3,0:T(8,128)} %bitcast.264, f32[1,16,4,16,16]{1,2,4,3,0:T(4,128)S(1)} %copy.227, f32[1,16,4,16,16]{1,2,4,3,0:T(4,128)S(1)} %copy.226, f32[1,16,4,16,16]{1,2,4,3,0:T(4,128)S(1)} %copy.225, f32[1,16,4,16,16]{1,2,4,3,0:T(4,128)S(1)} %copy.224), kind=kOutput, calls=%fused_computation.23 | convolution fusion | flops 13041664 | bytes 1572864 | tf_op jit(solution)/shard_map/bizxy,bioxy->bozxy/dot_general | solution.py:151
  150.9 4.8 collective-permute-done.4
  156.7 4.0 collective-permute-done.5
  162.3 4.4 copy.241
  166.7 4.8 bitcast_bitcast_fusion.1
  171.5 3.5 reshape.88
  175.0 22.0 %all_to_all.72 = f32[32,1,4096]{2,1,0:T(1,128)S(1)} all-to-all(f32[32,1,4096]{2,1,0:T(1,128)S(1)} %reshape.88), channel_id=1, replica_groups=mesh['gx'=8,'gy'=32] {'gy'}, dimensions={0} | all-to-all | bytes 1048576 | tf_op jit(solution)/shard_map/all_to_all | solution.py:168
  199.0 2.8 reshape.89
  201.8 4.7 copy.242
  206.5 2.8 copy.243
  209.4 4.4 collective-permute-done.6
  214.9 2.2 collective-permute-start.7
  217.2 2.8 fusion.27
  220.1 15.0 %collective-permute-done.7 = f32[16,32,3,128]{3,1,2,0:T(8,128)S(1)} collective-permute-done((f32[16,32,3,128]{3,1,2,0:T(8,128)S(1)}, f32[16,32,3,128]{3,1,2,0:T(8,128)S(1)}, u32[]{:S(2)}, u32[]{:S(2)}) %collective-permute-start.7) | collective-permute-done | bytes 786464 | tf_op jit(solution)/shard_map/ppermute | solution.py:24
  235.3 6.6 %fusion.1133 = (f32[16]{0:T(128)}, f32[16,32,8,128]{3,2,1,0:T(8,128)S(1)}, f32[16,32,8,128]{3,2,1,0:T(8,128)}) fusion(f32[16,32,8,128]{3,2,1,0:T(8,128)S(1)} %copy-done.20, f32[16]{0:T(128)S(1)} %copy-done.21, f32[16,32,8,128]{3,0,2,1:T(8,128)S(1)} %fusion.27, f32[16,32,8,128]{3,2,1,0:T(8,128)S(1)} %copy-done.1, s32[7]{0:T(128)S(1)} %iota_multiply_fusion.2, ...), kind=kOutput, calls=%fused_computation.1198 | convolution fusion | flops 56100200 | bytes 12320924 | tf_op jit(solution)/shard_map/kr,axrs->axks/dot_general | solution.py:54
  241.9 5.3 collective-permute-done.8
  247.4 2.0 fusion.33
  249.6 19.6 %collective-permute-done.9 = f32[16,16,6,128]{3,1,2,0:T(8,128)S(1)} collective-permute-done((f32[16,16,6,128]{3,1,2,0:T(8,128)S(1)}, f32[16,16,6,128]{3,1,2,0:T(8,128)S(1)}, u32[]{:S(2)}, u32[]{:S(2)}) %collective-permute-start.9) | collective-permute-done | bytes 786464 | tf_op jit(solution)/shard_map/ppermute | solution.py:24
  269.3 2.1 fusion.42
  271.5 4.4 copy.251
  275.9 3.5 reshape.90
  279.4 19.5 %all_to_all.73 = f32[32,1,4096]{2,1,0:T(1,128)S(1)} all-to-all(f32[32,1,4096]{2,1,0:T(1,128)S(1)} %reshape.90), channel_id=1, replica_groups=mesh['gx'=8,'gy'=32] {'gy'}, dimensions={0} | all-to-all | bytes 1048576 | tf_op jit(solution)/shard_map/all_to_all | solution.py:127
  300.8 2.8 reshape.91
  303.6 4.8 copy.253
  308.4 3.7 copy.254
  312.2 3.9 collective-permute-done.10
  319.1 5.1 collective-permute-done.11
  325.1 17.3 %all_gather.7 = f32[64,32,32]{0,2,1:T(8,128)S(1)} all-gather(f32[64,4,32]{0,2,1:T(8,128)S(1)} %fusion.119), channel_id=1, replica_groups=mesh['gx'=8,'gy'=32] {'gx'}, dimensions={1}, use_global_device_ids=true | all-gather | bytes 294912 | tf_op jit(solution)/shard_map/all_gather | solution.py:142
  350.4 18.2 %bitcast_subtract_fusion = f32[4,16,4,16,16]{1,2,4,3,0:T(4,128)S(1)} fusion(f32[4,16,16,16,16]{2,1,4,3,0:T(8,128)} %bitcast.265, f32[1,16,4,16,16]{1,2,4,3,0:T(4,128)} %copy.269, f32[1,16,4,16,16]{1,2,4,3,0:T(4,128)} %copy.268, f32[1,16,4,16,16]{1,2,4,3,0:T(4,128)} %copy.267, f32[1,16,4,16,16]{1,2,4,3,0:T(4,128)S(1)} %copy.266), kind=kOutput, calls=%fused_computation.19 | convolution fusion | flops 13041664 | bytes 1572864 | tf_op jit(solution)/shard_map/bozxy,bioxy->bizxy/dot_general | solution.py:147
  384.9 4.8 collective-permute-done.12
  390.7 4.0 collective-permute-done.13
  396.3 4.4 copy.283
  400.7 4.7 bitcast_bitcast_fusion
  405.5 4.2 reshape.92
  409.7 5.7 all-to-all-start.3
  415.5 17.6 %fusion.86 = f32[4,16,16,16,16]{4,3,2,1,0:T(8,128)} fusion(f32[1,16,4,16,16]{1,2,4,3,0:T(4,128)} %copy.269, f32[1,16,4,16,16]{1,2,4,3,0:T(4,128)} %copy.268, f32[1,16,4,16,16]{1,2,4,3,0:T(4,128)} %copy.267, f32[1,16,4,16,16]{1,2,4,3,0:T(4,128)} %copy-done.10, f32[1,16,4,16,16]{1,2,4,3,0:T(4,128)} %copy-done.9, f32[1,16,4,16,16]{1,2,4,3,0:T(4,128)} %copy-done.7, ...), kind=kOutput, calls=%fused_computation.106 | convolution fusion | flops 12976128 | bytes 1572864 | tf_op jit(solution)/shard_map/bizxy,bozxy->bioxy/dot_general | solution.py:201
  433.0 7.7 %copy.290 = f32[4,16,16,256]{3,2,1,0:T(8,128)} copy(f32[4,16,16,256]{1,2,3,0:T(8,128)} %bitcast.266) | data formatting | bytes 2097152 | tf_op jit(solution)/shard_map/reshape | solution.py:204
  440.8 6.3 %fusion.45 = f32[16,16]{0,1:T(8,128)S(1)} fusion(f32[16,32,8,128]{3,2,1,0:T(8,128)} %param.5, f32[16,32,8,128]{3,2,1,0:T(8,128)S(1)} %get-tuple-element.28), kind=kOutput, calls=%fused_computation.66 | convolution fusion | flops 100663296 | bytes 4195328 | tf_op jit(solution)/shard_map/ixys,oxys->io/dot_general | solution.py:206
  447.1 77.5 %all-reduce = (f32[16,16]{0,1:T(8,128)S(1)}, f32[16]{0:T(128)S(1)}) all-reduce(f32[16,16]{0,1:T(8,128)S(1)} %fusion.45, f32[16]{0:T(128)S(1)} %copy-done.19), channel_id=1, replica_groups=mesh['gx'=8,'gy'=32] {'gx','gy'}, use_global_device_ids=true, to_apply=%region_1.2 | all-reduce | flops 272 | bytes 2176 | tf_op jit(solution)/shard_map/psum | solution.py:210
  526.5 2.8 reshape.93
  529.3 4.8 copy.284
  534.1 2.8 copy.285
  537.7 4.1 collective-permute-done.14
  541.8 2.2 convolution_bitcast_fusion
  547.0 4.4 fusion.24
  551.4 41.4 %all-reduce.3.cloned.1.call-done = f32[4,16,16,256]{3,2,1,0:T(8,128)} async-done(((f32[4,16,16,256]{3,2,1,0:T(8,128)}), f32[4,16,16,256]{3,2,1,0:T(8,128)}) %all-reduce.3.cloned.1.call-update) | async-done | bytes 1048592 | tf_op jit(solution)/shard_map/psum | solution.py:205
  592.8 2.3 broadcast_multiply_fusion
  596.9 5.2 bitcast_add_fusion
  (169 shorter events, 71.7 us)
Async XLA Ops:
  7.2 210.0 %copy-start = (f32[16,16]{1,0:T(8,128)S(1)}, f32[16,16]{1,0:T(8,128)}, u32[]{:S(2)}) copy-start(f32[16,16]{1,0:T(8,128)} %param.8) | copy-start | bytes 3076
  9.2 6.7 %collective-permute-start = (f32[16,6,8,128]{3,1,2,0:T(8,128)S(1)}, f32[16,6,8,128]{3,1,2,0:T(8,128)S(1)}, u32[]{:S(2)}, u32[]{:S(2)}) collective-permute-start(f32[16,6,8,128]{3,1,2,0:T(8,128)S(1)} %slice.104), channel_id=1, source_target_pairs={{0,224},{32,0},{64,32},{96,64},{128,96},{160,128},{192,160},{224,1... | collective-permute-start | bytes 1179656 | tf_op jit(solution)/shard_map/ppermute | solution.py:24
  17.9 25.2 %collective-permute-start.1 = (f32[16,16,6,128]{3,1,2,0:T(8,128)S(1)}, f32[16,16,6,128]{3,1,2,0:T(8,128)S(1)}, u32[]{:S(2)}, u32[]{:S(2)}) collective-permute-start(f32[16,16,6,128]{3,1,2,0:T(8,128)S(1)} %slice.105), channel_id=1, source_target_pairs={{0,31},{1,0},{2,1},{3,2},{4,3},{5,4},{6,5},{7,6},{8,7},{9,8},{10,9... | collective-permute-start | bytes 2359304 | tf_op jit(solution)/shard_map/ppermute | solution.py:24
  49.8 12.0 %copy-start.4 = (f32[4,16,16,256]{3,2,1,0:T(8,128)S(1)}, f32[4,16,16,256]{3,2,1,0:T(8,128)}, u32[]{:S(2)}) copy-start(f32[4,16,16,256]{3,2,1,0:T(8,128)} %param.7) | copy-start | bytes 3145732
  54.1 25.3 %all-to-all-start = ((f32[32,1,4096]{2,1,0:T(1,128)}), f32[32,1,4096]{2,1,0:T(1,128)S(1)}, u32[]{:S(2)}, u32[]{:S(2)}) async-start(f32[32,1,4096]{2,1,0:T(1,128)} %reshape.86), calls=%async_computation | async-start | bytes 1048576 | tf_op jit(solution)/shard_map/all_to_all | solution.py:127
  93.2 3.9 collective-permute-start.2
  98.2 5.8 collective-permute-start.3
  100.1 224.6 %copy-start.15 = (s32[32]{0:T(128)}, s32[32]{0:T(128)S(1)}, u32[]{:S(2)}) copy-start(s32[32]{0:T(128)S(1)} %iota_multiply_fusion.3) | copy-start | bytes 388
  122.9 2.0 copy-start.5
  123.5 1.3 copy-start.7
  124.2 0.8 copy-start.8
  124.8 0.8 copy-start.9
  150.8 5.0 collective-permute-start.4
  150.9 84.3 %copy-start.11 = (s32[7]{0:T(128)}, s32[7]{0:T(128)S(1)}, u32[]{:S(2)}) copy-start(s32[7]{0:T(128)S(1)} %iota_multiply_fusion.2) | copy-start | bytes 88
  156.7 4.1 collective-permute-start.5
  156.7 10.0 %copy-start.17 = (s32[11]{0:T(128)}, s32[11]{0:T(128)S(1)}, u32[]{:S(2)}) copy-start(s32[11]{0:T(128)S(1)} %iota_multiply_fusion.1) | copy-start | bytes 136
  209.3 7.9 %copy-start.1 = (f32[16,32,8,128]{3,2,1,0:T(8,128)S(1)}, f32[16,32,8,128]{3,2,1,0:T(8,128)}, u32[]{:S(2)}) copy-start(f32[16,32,8,128]{3,2,1,0:T(8,128)} %param.5) | copy-start | bytes 6291460
  209.3 4.4 collective-permute-start.6
  209.4 10.7 %copy-start.13 = (s32[19]{0:T(128)}, s32[19]{0:T(128)S(1)}, u32[]{:S(2)}) copy-start(s32[19]{0:T(128)S(1)} %iota_multiply_fusion) | copy-start | bytes 232
  214.9 20.2 %collective-permute-start.7 = (f32[16,32,3,128]{3,1,2,0:T(8,128)S(1)}, f32[16,32,3,128]{3,1,2,0:T(8,128)S(1)}, u32[]{:S(2)}, u32[]{:S(2)}) collective-permute-start(f32[16,32,3,128]{3,1,2,0:T(8,128)S(1)} %slice.115), channel_id=1, source_target_pairs={{0,1},{1,2},{2,3},{3,4},{4,5},{5,6},{6,7},{7,8},{8,9},{9,10},{10,1... | collective-permute-start | bytes 2359304 | tf_op jit(solution)/shard_map/ppermute | solution.py:24
  220.0 15.2 %copy-start.20 = (f32[16,32,8,128]{3,2,1,0:T(8,128)S(1)}, f32[16,32,8,128]{3,2,1,0:T(8,128)}, u32[]{:S(2)}) copy-start(f32[16,32,8,128]{3,2,1,0:T(8,128)} %param.6) | copy-start | bytes 6291460
  220.0 15.2 %copy-start.21 = (f32[16]{0:T(128)S(1)}, f32[16]{0:T(128)}, u32[]{:S(2)}) copy-start(f32[16]{0:T(128)} %param.9) | copy-start | bytes 196
  241.9 5.3 collective-permute-start.8
  249.5 19.7 %collective-permute-start.9 = (f32[16,16,6,128]{3,1,2,0:T(8,128)S(1)}, f32[16,16,6,128]{3,1,2,0:T(8,128)S(1)}, u32[]{:S(2)}, u32[]{:S(2)}) collective-permute-start(f32[16,16,6,128]{3,1,2,0:T(8,128)S(1)} %slice.117), channel_id=1, source_target_pairs={{0,31},{1,0},{2,1},{3,2},{4,3},{5,4},{6,5},{7,6},{8,7},{9,8},{10,9... | collective-permute-start | bytes 2359304 | tf_op jit(solution)/shard_map/ppermute | solution.py:24
  312.2 3.9 collective-permute-start.10
  317.2 7.0 %collective-permute-start.11 = (f32[64,6,64]{2,1,0:T(8,128)S(1)}, f32[64,6,64]{2,1,0:T(8,128)S(1)}, u32[]{:S(2)}, u32[]{:S(2)}) collective-permute-start(f32[64,6,64]{2,1,0:T(8,128)S(1)} %bitcast.290), channel_id=1, source_target_pairs={{0,224},{32,0},{64,32},{96,64},{128,96},{160,128},{192,160},{224,1... | collective-permute-start | bytes 294920 | tf_op jit(solution)/shard_map/ppermute | solution.py:24
  346.1 4.4 copy-start.10
  379.3 10.5 %copy-start.12 = (s32[7]{0:T(128)S(1)}, s32[7]{0:T(128)}, u32[]{:S(2)}) copy-start(s32[7]{0:T(128)} %copy-done.11) | copy-start | bytes 88
  379.3 10.8 %copy-start.16 = (s32[32]{0:T(128)S(1)}, s32[32]{0:T(128)}, u32[]{:S(2)}) copy-start(s32[32]{0:T(128)} %copy-done.15) | copy-start | bytes 388
  381.4 13.4 %copy-start.18 = (s32[11]{0:T(128)S(1)}, s32[11]{0:T(128)}, u32[]{:S(2)}) copy-start(s32[11]{0:T(128)} %copy-done.17) | copy-start | bytes 136
  384.8 5.0 collective-permute-start.12
  390.7 4.1 collective-permute-start.13
  405.5 10.0 %copy-start.6 = (f32[1,16,4,16,16]{1,2,4,3,0:T(4,128)S(1)}, f32[1,16,4,16,16]{1,2,4,3,0:T(4,128)}, u32[]{:S(2)}) copy-start(f32[1,16,4,16,16]{1,2,4,3,0:T(4,128)} %copy-done.5) | copy-start | bytes 196612
  409.7 114.9 %all-to-all-start.3 = ((f32[32,1,4096]{2,1,0:T(1,128)}), f32[32,1,4096]{2,1,0:T(1,128)S(1)}, u32[]{:S(2)}, u32[]{:S(2)}) async-start(f32[32,1,4096]{2,1,0:T(1,128)} %reshape.92), calls=%async_computation.3 | async-start | bytes 1048576 | tf_op jit(solution)/shard_map/all_to_all | solution.py:168
  415.4 177.4 %all-reduce.3.cloned.1.call-start = ((), (), s32[]{:S(2)}) async-start(), calls=%async_computation.4 | async-start | bytes 2097152 | tf_op jit(solution)/shard_map/psum | solution.py:205
  440.8 6.3 %copy-start.19 = (f32[16]{0:T(128)S(1)}, f32[16]{0:T(128)}, u32[]{:S(2)}) copy-start(f32[16]{0:T(128)} %get-tuple-element.27) | copy-start | bytes 196
  534.1 7.7 %copy-start.14 = (s32[19]{0:T(128)S(1)}, s32[19]{0:T(128)}, u32[]{:S(2)}) copy-start(s32[19]{0:T(128)} %copy-done.13) | copy-start | bytes 232
  536.9 0.8 copy-start.3
  536.9 4.9 collective-permute-start.14
  545.0 50.1 %collective-permute-start.15 = (f32[16,32,3,128]{3,1,2,0:T(8,128)}, f32[16,32,3,128]{3,1,2,0:T(8,128)}, u32[]{:S(2)}, u32[]{:S(2)}) collective-permute-start(f32[16,32,3,128]{3,1,2,0:T(8,128)} %slice.127), channel_id=1, source_target_pairs={{0,1},{1,2},{2,3},{3,4},{4,5},{5,6},{6,7},{7,8},{8,9},{9,10},{10,1... | collective-permute-start | bytes 2359304 | tf_op jit(solution)/shard_map/ppermute | solution.py:24
  595.1 1.8 copy-start.2
Sparse Core Ops, SparseCore 0:
  440.9 151.8 all-reduce.2
where the time goes:
time: 616 us; the launch traced here: 609 us
  waiting for transfers between devices  159 us (26%)
  blocking collectives  151 us (25%)
  local copies, waits for them, and re-layouts  122 us (20%)
  matrix products  119 us (19%)
  starting transfers between devices  29.7 us (5%)
  between operations  15.3 us (2%)
  other arithmetic  13.7 us (2%)
    ppermute x16, waiting for transfers between devices, from_behind(): lax.ppermute(value, axis, [(i, (i + by) % devices) for i in range(devices)])  106 us
    psum x1, blocking collectives, local(): point_total, bias_total = lax.psum((point_local, bias_local), ('gx', 'gy'))  77.5 us
    psum x1, waiting for transfers between devices, local(): mode_total = lax.psum(mode_local, 'gy')  41.4 us
    unnamed x56, local copies, waits for them, and re-layouts  40.1 us
    all_gather x2, blocking collectives, wave_block(): gathered = lax.all_gather(level_three, 'gx', axis=1, tiled=True)  31.6 us
    all_to_all x1, blocking collectives, wave_block(): lax.all_to_all(from_lanes(delta_one, channels), 'gy', split_axis=2, conca...  22 us
    dot_general x24, matrix products, plane_y(): jnp.einsum('kr,axr->axk', matrix, signal, precision=lax.Precision.HIGHEST)  20.3 us
    all_to_all x1, blocking collectives, wave_block(): lax.all_to_all(level_one, 'gy', split_axis=3, concat_axis=2, tiled=True)  19.5 us
  transfers between devices with their start and end apart: 19, of which 17 were waited for; matrix products, arithmetic and copies ran while one was open for 11% of the time, Pallas kernels for 0%

commit v1 on v0

--- a/solution.py
+++ b/solution.py
@@ -202,7 +202,7 @@
         "bizxy,bozxy->bioxy", bands_flow, bands_grad, precision=lax.Precision.HIGHEST
     )
     mode_local = mode_local.reshape(4, channels, channels, modes_x * modes_y)
-    mode_total = lax.psum(mode_local, "gy")
+    mode_total = jnp.sum(lax.all_gather(mode_local, "gy"), axis=0)
     point_local = jnp.einsum(
         "ixys,oxys->io", flow_field, grad_inner, precision=lax.Precision.HIGHEST
     )

time: 616 us -> 680 us (1.10)
  blocking collectives: 151 us -> 179 us
  other arithmetic: 13.7 us -> 30.2 us
  local copies, waits for them, and re-layouts: 122 us -> 137 us
  waiting for transfers between devices: 159 us -> 169 us
    all_gather x0 -> x1, waiting for transfers between devices: none -> 51.7 us  [local(): mode_total = jnp.sum(lax.all_gather(mode_local, 'gy'), axis=0)]
    psum x1 -> x0, waiting for transfers between devices: 41.4 us -> none  [local(): mode_total = lax.psum(mode_local, 'gy')]
    all_to_all x1 -> x2, blocking collectives: 22 us -> 48.5 us  [wave_block(): lax.all_to_all(from_lanes(delta_one, channels), 'gy', split_axis=2, conca...]
    unnamed x56 -> x44, local copies, waits for them, and re-layouts: 40.1 us -> 53.5 us
    reduce_sum x0 -> x1, other arithmetic: none -> 12.3 us  [local(): mode_total = jnp.sum(lax.all_gather(mode_local, 'gy'), axis=0)]
    reshape x1 -> x0, local copies, waits for them, and re-layouts: 7.74 us -> none  [local(): mode_local = mode_local.reshape(4, channels, channels, modes_x * modes_y)]
    another operation x0 -> x1, local copies, waits for them, and re-layouts: none -> 7.47 us  [local(): mode_total = jnp.sum(lax.all_gather(mode_local, 'gy'), axis=0)]
  transfers between devices with their start and end apart: 19 -> 18, of which waited for: 17 -> 17; matrix products, arithmetic and copies ran while one was open for 11% -> 13% of each run, Pallas kernels for 0% -> 0%
where the time goes in v1:
time: 680 us; the launch traced here: 671 us
  blocking collectives  179 us (26%)
  waiting for transfers between devices  169 us (25%)
  local copies, waits for them, and re-layouts  137 us (20%)
  matrix products  115 us (17%)
  other arithmetic  30.2 us (4%)
  starting transfers between devices  25 us (4%)
  between operations  15.5 us (2%)
    ppermute x16, waiting for transfers between devices, from_behind(): lax.ppermute(value, axis, [(i, (i + by) % devices) for i in range(devices)])  106 us
    psum x1, blocking collectives, local(): point_total, bias_total = lax.psum((point_local, bias_local), ('gx', 'gy'))  79 us
    unnamed x44, local copies, waits for them, and re-layouts  53.5 us
    all_gather x1, waiting for transfers between devices, local(): mode_total = jnp.sum(lax.all_gather(mode_local, 'gy'), axis=0)  51.7 us
    all_to_all x2, blocking collectives, wave_block(): lax.all_to_all(from_lanes(delta_one, channels), 'gy', split_axis=2, conca...  48.5 us
    all_gather x2, blocking collectives, wave_block(): gathered = lax.all_gather(level_three, 'gx', axis=1, tiled=True)  31.8 us
    dot_general x24, matrix products, plane_y(): jnp.einsum('kr,axr->axk', matrix, signal, precision=lax.Precision.HIGHEST)  21.5 us
    all_to_all x1, blocking collectives, wave_block(): lax.all_to_all(level_one, 'gy', split_axis=3, concat_axis=2, tiled=True)  19.5 us
  transfers between devices with their start and end apart: 18, of which 17 were waited for; matrix products, arithmetic and copies ran while one was open for 13% of the time, Pallas kernels for 0%

profile of v1, /device:TPU:8, one launch (start us, length us, event | category | flops | bytes accessed | tf_op | source)
XLA Modules:
  0.0 670.9 jit_solution(11738014585423525236)
XLA Ops:
  9.3 6.7 collective-permute-done
  17.9 8.1 %collective-permute-start.1 = (f32[16,16,6,128]{3,1,2,0:T(8,128)S(1)}, f32[16,16,6,128]{3,1,2,0:T(8,128)S(1)}, u32[]{:S(2)}, u32[]{:S(2)}) collective-permute-start(f32[16,16,6,128]{3,1,2,0:T(8,128)S(1)} %slice.105), channel_id=1, source_target_pairs={{0,31},{1,0},{2,1},{3,2},{4,3},{5,4},{6,5},{7,6},{8,7},{9,8},{10,9... | collective-permute-start | bytes 2359304 | tf_op jit(solution)/shard_map/ppermute | solution.py:24
  26.0 17.1 %collective-permute-done.1 = f32[16,16,6,128]{3,1,2,0:T(8,128)S(1)} collective-permute-done((f32[16,16,6,128]{3,1,2,0:T(8,128)S(1)}, f32[16,16,6,128]{3,1,2,0:T(8,128)S(1)}, u32[]{:S(2)}, u32[]{:S(2)}) %collective-permute-start.1) | collective-permute-done | bytes 786464 | tf_op jit(solution)/shard_map/ppermute | solution.py:24
  45.4 4.4 copy.209
  49.8 4.3 reshape.82
  54.1 7.5 %all-to-all-start = ((f32[32,1,4096]{2,1,0:T(1,128)}), f32[32,1,4096]{2,1,0:T(1,128)S(1)}, u32[]{:S(2)}, u32[]{:S(2)}) async-start(f32[32,1,4096]{2,1,0:T(1,128)} %reshape.82), calls=%async_computation | async-start | bytes 1048576 | tf_op jit(solution)/shard_map/all_to_all | solution.py:127
  61.8 6.2 copy.306
  68.0 11.2 %all-to-all-done = f32[32,1,4096]{2,1,0:T(1,128)S(1)} async-done(((f32[32,1,4096]{2,1,0:T(1,128)}), f32[32,1,4096]{2,1,0:T(1,128)S(1)}, u32[]{:S(2)}, u32[]{:S(2)}) %all-to-all-start) | async-done | bytes 524320 | tf_op jit(solution)/shard_map/all_to_all | solution.py:127
  81.7 2.8 reshape.83
  84.4 4.8 copy.211
  89.3 3.7 copy.212
  93.1 3.9 collective-permute-done.2
  99.9 3.9 collective-permute-done.3
  104.8 14.5 %all_gather.9 = f32[64,32,32]{0,2,1:T(8,128)S(1)} all-gather(f32[64,4,32]{0,2,1:T(8,128)S(1)} %fusion.123), channel_id=1, replica_groups=mesh['gx'=8,'gy'=32] {'gx'}, dimensions={1}, use_global_device_ids=true | all-gather | bytes 294912 | tf_op jit(solution)/shard_map/all_gather | solution.py:142
  125.7 14.6 %bitcast_subtract_fusion.1 = f32[4,16,4,16,16]{1,2,4,3,0:T(4,128)S(1)} fusion(f32[4,16,16,16,16]{2,1,4,3,0:T(8,128)} %bitcast.264, f32[1,16,4,16,16]{1,2,4,3,0:T(4,128)S(1)} %copy.227, f32[1,16,4,16,16]{1,2,4,3,0:T(4,128)S(1)} %copy.226, f32[1,16,4,16,16]{1,2,4,3,0:T(4,128)S(1)} %copy.225, f32[1,16,4,16,16]{1,2,4,3,0:T(4,128)S(1)} %copy.224), kind=kOutput, calls=%fused_computation.24 | convolution fusion | flops 13041664 | bytes 1572864 | tf_op jit(solution)/shard_map/bizxy,bioxy->bozxy/dot_general | solution.py:151
  150.8 4.8 collective-permute-done.4
  156.5 4.0 collective-permute-done.5
  162.1 4.4 copy.241
  166.6 4.7 bitcast_bitcast_fusion.1
  171.3 3.5 reshape.84
  174.8 22.1 %all_to_all.72 = f32[32,1,4096]{2,1,0:T(1,128)S(1)} all-to-all(f32[32,1,4096]{2,1,0:T(1,128)S(1)} %reshape.84), channel_id=1, replica_groups=mesh['gx'=8,'gy'=32] {'gy'}, dimensions={0} | all-to-all | bytes 1048576 | tf_op jit(solution)/shard_map/all_to_all | solution.py:168
  198.8 2.8 reshape.85
  201.6 4.8 copy.242
  206.3 2.8 copy.243
  209.2 4.4 collective-permute-done.6
  217.0 2.8 fusion.27
  219.9 15.0 %collective-permute-done.7 = f32[16,32,3,128]{3,1,2,0:T(8,128)S(1)} collective-permute-done((f32[16,32,3,128]{3,1,2,0:T(8,128)S(1)}, f32[16,32,3,128]{3,1,2,0:T(8,128)S(1)}, u32[]{:S(2)}, u32[]{:S(2)}) %collective-permute-start.7) | collective-permute-done | bytes 786464 | tf_op jit(solution)/shard_map/ppermute | solution.py:24
  235.1 6.3 fusion.1133
  241.5 5.3 collective-permute-done.8
  249.1 19.6 %collective-permute-done.9 = f32[16,16,6,128]{3,1,2,0:T(8,128)S(1)} collective-permute-done((f32[16,16,6,128]{3,1,2,0:T(8,128)S(1)}, f32[16,16,6,128]{3,1,2,0:T(8,128)S(1)}, u32[]{:S(2)}, u32[]{:S(2)}) %collective-permute-start.9) | collective-permute-done | bytes 786464 | tf_op jit(solution)/shard_map/ppermute | solution.py:24
  271.0 4.4 copy.251
  275.4 3.5 reshape.86
  278.9 19.5 %all_to_all.73 = f32[32,1,4096]{2,1,0:T(1,128)S(1)} all-to-all(f32[32,1,4096]{2,1,0:T(1,128)S(1)} %reshape.86), channel_id=1, replica_groups=mesh['gx'=8,'gy'=32] {'gy'}, dimensions={0} | all-to-all | bytes 1048576 | tf_op jit(solution)/shard_map/all_to_all | solution.py:127
  300.3 2.8 reshape.87
  303.1 4.8 copy.253
  307.9 3.7 copy.254
  311.7 3.9 collective-permute-done.10
  318.6 5.1 collective-permute-done.11
  324.6 17.3 %all_gather.10 = f32[64,32,32]{0,2,1:T(8,128)S(1)} all-gather(f32[64,4,32]{0,2,1:T(8,128)S(1)} %fusion.119), channel_id=1, replica_groups=mesh['gx'=8,'gy'=32] {'gx'}, dimensions={1}, use_global_device_ids=true | all-gather | bytes 294912 | tf_op jit(solution)/shard_map/all_gather | solution.py:142
  350.7 17.8 %fusion.86 = f32[4,16,16,16,16]{4,3,2,1,0:T(8,128)} fusion(f32[1,16,4,16,16]{1,2,4,3,0:T(4,128)} %copy.269, f32[1,16,4,16,16]{1,2,4,3,0:T(4,128)} %copy.268, f32[1,16,4,16,16]{1,2,4,3,0:T(4,128)} %copy.267, f32[1,16,4,16,16]{1,2,4,3,0:T(4,128)} %copy.266, f32[1,16,4,16,16]{1,2,4,3,0:T(4,128)} %copy-done.8, f32[1,16,4,16,16]{1,2,4,3,0:T(4,128)} %copy-done.10, ...), kind=kOutput, calls=%fused_computation.106 | convolution fusion | flops 12976128 | bytes 1572864 | tf_op jit(solution)/shard_map/bizxy,bozxy->bioxy/dot_general | solution.py:201
  368.4 7.5 %copy.290 = f32[1,4,16,16,256]{4,3,2,1,0:T(8,128)} copy(f32[1,4,16,16,256]{2,3,4,1,0:T(8,128)} %bitcast.266) | data formatting | bytes 2097152 | tf_op jit(solution)/shard_map/all_gather;reshape | solution.py:205
  375.9 17.3 %bitcast_subtract_fusion = f32[4,16,4,16,16]{1,2,4,3,0:T(4,128)S(1)} fusion(f32[4,16,16,16,16]{2,1,4,3,0:T(8,128)} %bitcast.265, f32[1,16,4,16,16]{1,2,4,3,0:T(4,128)S(1)} %copy-done.12, f32[1,16,4,16,16]{1,2,4,3,0:T(4,128)} %copy.268, f32[1,16,4,16,16]{1,2,4,3,0:T(4,128)S(1)} %copy-done.11, f32[1,16,4,16,16]{1,2,4,3,0:T(4,128)} %copy.266), kind=kOutput, calls=%fused_computation.20 | convolution fusion | flops 13041664 | bytes 1572864 | tf_op jit(solution)/shard_map/bozxy,bioxy->bizxy/dot_general | solution.py:147
  398.7 2.3 copy.271
  401.0 2.7 fusion.70
  410.4 4.8 collective-permute-done.12
  416.2 4.0 collective-permute-done.13
  421.8 4.5 copy.283
  426.2 4.9 bitcast_bitcast_fusion
  431.1 3.5 reshape.88
  434.6 26.4 %all_to_all.74 = f32[32,1,4096]{2,1,0:T(1,128)S(1)} all-to-all(f32[32,1,4096]{2,1,0:T(1,128)S(1)} %reshape.88), channel_id=1, replica_groups=mesh['gx'=8,'gy'=32] {'gy'}, dimensions={0} | all-to-all | bytes 1048576 | tf_op jit(solution)/shard_map/all_to_all | solution.py:168
  463.0 2.9 reshape.89
  465.8 4.9 copy.284
  470.8 2.8 copy.285
  474.4 3.7 collective-permute-done.14
  481.2 2.5 collective-permute-start.15
  483.7 4.8 fusion.45
  488.5 79.0 %all-reduce = (f32[16,16]{0,1:T(8,128)S(1)}, f32[16]{0:T(128)S(1)}) all-reduce(f32[16,16]{0,1:T(8,128)S(1)} %fusion.45, f32[16]{0:T(128)S(1)} %get-tuple-element.27), channel_id=1, replica_groups=mesh['gx'=8,'gy'=32] {'gx','gy'}, use_global_device_ids=true, to_apply=%region_1.2 | all-reduce | flops 272 | bytes 2176 | tf_op jit(solution)/shard_map/psum | solution.py:210
  568.7 3.1 fusion.24
  573.2 5.2 bitcast_add_fusion
  578.4 51.7 %all-gather.2.cloned.1.call-done = f32[32,4,16,16,256]{4,3,2,1,0:T(8,128)} async-done(((f32[1,4,16,16,256]{4,3,2,1,0:T(8,128)}), f32[32,4,16,16,256]{4,3,2,1,0:T(8,128)}) %all-gather.2.cloned.1.call-update) | async-done | bytes 33554448 | tf_op jit(solution)/shard_map/all_gather | solution.py:205
  630.2 12.3 %reduce_sum.18 = f32[4,16,16,256]{3,2,1,0:T(8,128)S(1)} reduce(f32[32,4,16,16,256]{4,3,2,1,0:T(8,128)} %all-gather.2.cloned.1.call-done, f32[]{:T(128)} %constant.348.clone.1), dimensions={0}, to_apply=%region_0.1 | reduce | flops 8126464 | bytes 34603012 | tf_op jit(solution)/shard_map/reduce_sum | solution.py:205
  642.5 6.3 copy.307
  648.8 7.5 %broadcast_multiply_fusion = f32[4,16,16,256]{1,2,3,0:T(8,128)} fusion(f32[4,16,16,256]{1,2,3,0:T(8,128)} %copy.307), kind=kLoop, calls=%fused_computation | loop fusion | flops 262144 | bytes 2097152 | tf_op jit(solution)/shard_map/div | solution.py:219
  656.3 7.4 %copy.294 = f32[4,16,16,256]{3,2,1,0:T(8,128)} copy(f32[4,16,16,256]{1,2,3,0:T(8,128)} %broadcast_multiply_fusion) | data formatting | bytes 2097152
  (157 shorter events, 79.8 us)
Async XLA Ops:
  7.2 209.9 %copy-start = (f32[16,16]{1,0:T(8,128)S(1)}, f32[16,16]{1,0:T(8,128)}, u32[]{:S(2)}) copy-start(f32[16,16]{1,0:T(8,128)} %param.8) | copy-start | bytes 3076
  9.2 6.7 %collective-permute-start = (f32[16,6,8,128]{3,1,2,0:T(8,128)S(1)}, f32[16,6,8,128]{3,1,2,0:T(8,128)S(1)}, u32[]{:S(2)}, u32[]{:S(2)}) collective-permute-start(f32[16,6,8,128]{3,1,2,0:T(8,128)S(1)} %slice.104), channel_id=1, source_target_pairs={{0,224},{32,0},{64,32},{96,64},{128,96},{160,128},{192,160},{224,1... | collective-permute-start | bytes 1179656 | tf_op jit(solution)/shard_map/ppermute | solution.py:24
  17.9 25.2 %collective-permute-start.1 = (f32[16,16,6,128]{3,1,2,0:T(8,128)S(1)}, f32[16,16,6,128]{3,1,2,0:T(8,128)S(1)}, u32[]{:S(2)}, u32[]{:S(2)}) collective-permute-start(f32[16,16,6,128]{3,1,2,0:T(8,128)S(1)} %slice.105), channel_id=1, source_target_pairs={{0,31},{1,0},{2,1},{3,2},{4,3},{5,4},{6,5},{7,6},{8,7},{9,8},{10,9... | collective-permute-start | bytes 2359304 | tf_op jit(solution)/shard_map/ppermute | solution.py:24
  49.8 12.0 %copy-start.5 = (f32[4,16,16,256]{3,2,1,0:T(8,128)S(1)}, f32[4,16,16,256]{3,2,1,0:T(8,128)}, u32[]{:S(2)}) copy-start(f32[4,16,16,256]{3,2,1,0:T(8,128)} %param.7) | copy-start | bytes 3145732
  54.1 25.1 %all-to-all-start = ((f32[32,1,4096]{2,1,0:T(1,128)}), f32[32,1,4096]{2,1,0:T(1,128)S(1)}, u32[]{:S(2)}, u32[]{:S(2)}) async-start(f32[32,1,4096]{2,1,0:T(1,128)} %reshape.82), calls=%async_computation | async-start | bytes 1048576 | tf_op jit(solution)/shard_map/all_to_all | solution.py:127
  61.6 568.6 %all-gather.2.cloned.1.call-start = ((), (), s32[]{:S(2)}) async-start(), calls=%async_computation.4 | async-start | bytes 34603008 | tf_op jit(solution)/shard_map/all_gather | solution.py:205
  93.0 3.9 collective-permute-start.2
  98.0 5.8 collective-permute-start.3
  122.9 2.0 copy-start.6
  123.5 1.3 copy-start.8
  124.2 0.8 copy-start.9
  124.9 0.8 copy-start.10
  150.6 5.0 collective-permute-start.4
  156.5 4.1 collective-permute-start.5
  209.1 7.9 %copy-start.1 = (f32[16,32,8,128]{3,2,1,0:T(8,128)S(1)}, f32[16,32,8,128]{3,2,1,0:T(8,128)}, u32[]{:S(2)}) copy-start(f32[16,32,8,128]{3,2,1,0:T(8,128)} %param.5) | copy-start | bytes 6291460
  209.2 4.4 collective-permute-start.6
  214.8 20.2 %collective-permute-start.7 = (f32[16,32,3,128]{3,1,2,0:T(8,128)S(1)}, f32[16,32,3,128]{3,1,2,0:T(8,128)S(1)}, u32[]{:S(2)}, u32[]{:S(2)}) collective-permute-start(f32[16,32,3,128]{3,1,2,0:T(8,128)S(1)} %slice.115), channel_id=1, source_target_pairs={{0,1},{1,2},{2,3},{3,4},{4,5},{5,6},{6,7},{7,8},{8,9},{9,10},{10,1... | collective-permute-start | bytes 2359304 | tf_op jit(solution)/shard_map/ppermute | solution.py:24
  219.9 15.2 %copy-start.13 = (f32[16,32,8,128]{3,2,1,0:T(8,128)S(1)}, f32[16,32,8,128]{3,2,1,0:T(8,128)}, u32[]{:S(2)}) copy-start(f32[16,32,8,128]{3,2,1,0:T(8,128)} %param.6) | copy-start | bytes 6291460
  219.9 15.2 %copy-start.14 = (f32[16]{0:T(128)S(1)}, f32[16]{0:T(128)}, u32[]{:S(2)}) copy-start(f32[16]{0:T(128)} %param.9) | copy-start | bytes 196
  241.4 5.3 collective-permute-start.8
  249.0 19.6 %collective-permute-start.9 = (f32[16,16,6,128]{3,1,2,0:T(8,128)S(1)}, f32[16,16,6,128]{3,1,2,0:T(8,128)S(1)}, u32[]{:S(2)}, u32[]{:S(2)}) collective-permute-start(f32[16,16,6,128]{3,1,2,0:T(8,128)S(1)} %slice.117), channel_id=1, source_target_pairs={{0,31},{1,0},{2,1},{3,2},{4,3},{5,4},{6,5},{7,6},{8,7},{9,8},{10,9... | collective-permute-start | bytes 2359304 | tf_op jit(solution)/shard_map/ppermute | solution.py:24
  311.6 3.9 collective-permute-start.10
  316.7 7.0 %collective-permute-start.11 = (f32[64,6,64]{2,1,0:T(8,128)S(1)}, f32[64,6,64]{2,1,0:T(8,128)S(1)}, u32[]{:S(2)}, u32[]{:S(2)}) collective-permute-start(f32[64,6,64]{2,1,0:T(8,128)S(1)} %bitcast.290), channel_id=1, source_target_pairs={{0,224},{32,0},{64,32},{96,64},{128,96},{160,128},{192,160},{224,1... | collective-permute-start | bytes 294920 | tf_op jit(solution)/shard_map/ppermute | solution.py:24
  346.6 4.0 copy-start.7
  368.4 7.5 %copy-start.11 = (f32[1,16,4,16,16]{1,2,4,3,0:T(4,128)S(1)}, f32[1,16,4,16,16]{1,2,4,3,0:T(4,128)}, u32[]{:S(2)}) copy-start(f32[1,16,4,16,16]{1,2,4,3,0:T(4,128)} %copy.267) | copy-start | bytes 196612
  368.4 7.5 %copy-start.12 = (f32[1,16,4,16,16]{1,2,4,3,0:T(4,128)S(1)}, f32[1,16,4,16,16]{1,2,4,3,0:T(4,128)}, u32[]{:S(2)}) copy-start(f32[1,16,4,16,16]{1,2,4,3,0:T(4,128)} %copy.269) | copy-start | bytes 196612
  401.0 5.1 copy-start.4
  410.2 5.0 collective-permute-start.12
  416.1 4.1 collective-permute-start.13
  473.6 0.8 copy-start.3
  473.6 10.1 %copy-start.2 = (f32[16,32,8,128]{3,2,1,0:T(8,128)S(1)}, f32[16,32,8,128]{3,2,1,0:T(8,128)}, u32[]{:S(2)}) copy-start(f32[16,32,8,128]{3,2,1,0:T(8,128)} %param.5) | copy-start | bytes 6291460
  473.6 4.4 collective-permute-start.14
  481.2 90.7 %collective-permute-start.15 = (f32[16,32,3,128]{3,1,2,0:T(8,128)}, f32[16,32,3,128]{3,1,2,0:T(8,128)}, u32[]{:S(2)}, u32[]{:S(2)}) collective-permute-start(f32[16,32,3,128]{3,1,2,0:T(8,128)} %slice.127), channel_id=1, source_target_pairs={{0,1},{1,2},{2,3},{3,4},{4,5},{5,6},{6,7},{7,8},{8,9},{9,10},{10,1... | collective-permute-start | bytes 2359304 | tf_op jit(solution)/shard_map/ppermute | solution.py:24
Sparse Core Ops, SparseCore 0:
  376.0 254.0 all-gather.1
